TPU v7x, 128 devices: a whole 4x4x4 slice. The times are simulated.
128 devices in a mesh: sec: 2 (over y_lo), dp: 16 (over z, y_hi, core), tensor: 4 (over x).
Axes of the slice: x: 4, y: 4 (y_hi: 2, y_lo: 2; y = y_hi * 2 + y_lo), z: 4, core: 2. Of those that a mesh axis runs over, the one named last changes fastest.
Arguments:
- student_rows: bfloat16 [2, 8192, 5376], P('sec', 'dp'), may hold values from -24 to 24
- teacher_rows: bfloat16 [2, 8192, 5376], P('sec', 'dp'), may hold values from -6 to 6
- norm_gain: float32 [5376], replicated, may hold values from 0.5 to 1.5
- post_gain: float32 [5376], replicated, may hold values from 0.5 to 1.5
- query_weight: bfloat16 [5376, 2048], P(('sec', 'dp'), 'tensor')
- key_weight: bfloat16 [5376, 1024], P(('sec', 'dp'), 'tensor')
- value_weight: bfloat16 [5376, 1024], P(('sec', 'dp'), 'tensor'), may hold values from -0.078125 to 0.078125
- out_weight: bfloat16 [5376, 2048], P(('sec', 'dp'), 'tensor'), may hold values from -0.125 to 0.125
Outputs:
- layer_output: bfloat16 [2, 8192, 5376], P('sec', 'dp', 'tensor')
- query_grad: float32 [5376, 2048], P(('sec', 'dp'), 'tensor')
- output_grad: float32 [5376, 2048], P(('sec', 'dp'), 'tensor')
All inputs are finite; a program needn't handle non-finite values.
Results may differ from a plain program's by a relative error of at most 0.025.
The roundings to bfloat16 on the way count: a program that leaves them out, or rounds other values in their place, can miss the bound.
Values may be sent and summed in bfloat16 or wider, within the bound.
A program may use at most 128 MiB of HBM per device.

v0:
```python
import math
import jax
import jax.numpy as jnp
from jax import lax
from jax.sharding import PartitionSpec as P

HEADS = 8
KV_HEADS = 4
HD = 256
W = 1024
norm_eps = 1e-06
rope_base = 10000.0
masked_score = -1e30


def from_partner(block, axis, bit):
    count = lax.axis_size(axis)
    route = []
    for low in range(count):
        high = low | 1 << bit
        if high != low and high < count:
            route += [(low, high), (high, low)]
    return lax.ppermute(block, axis, route)


def from_behind(x, axis, by):
    count = lax.axis_size(axis)
    pairs = [(i, i + by) for i in range(count) if 0 <= i + by < count]
    return lax.ppermute(x, axis, pairs)


def rotate(values, cos_table, sin_table, sign_value):
    row_count = values.shape[0]
    half_dim = cos_table.shape[1]
    per_head = values.reshape(row_count, -1, 2 * half_dim)
    leading = per_head[:, :, :half_dim]
    trailing = per_head[:, :, half_dim:]
    cosines = cos_table[:, None, :]
    sin_scaled = sign_value * sin_table[:, None, :]
    rotated = jnp.concatenate(
        [leading * cosines - trailing * sin_scaled, trailing * cosines + leading * sin_scaled],
        axis=2,
    )
    return rotated.reshape(row_count, -1)


def shards(
    student_rows,
    teacher_rows,
    norm_gain,
    post_gain,
    query_weight,
    key_weight,
    value_weight,
    out_weight,
):
    tok_count = student_rows.shape[1]
    model_width = student_rows.shape[2]
    tensor_count = lax.axis_size("tensor")
    share_cols = model_width // tensor_count
    data_count = lax.axis_size("sec") * lax.axis_size("dp")
    blocks_back = (W + tok_count - 1) // tok_count
    key_count = (blocks_back + 1) * tok_count
    local_groups = key_weight.shape[1] // HD
    group_size = HEADS // KV_HEADS
    query_cols = query_weight.shape[1]
    score_scale = 1.0 / math.sqrt(HD)
    loss_scale = 2.0 / math.sqrt(data_count * tok_count)
    target = from_partner(teacher_rows[0], "sec", 0)
    query_full, key_full, value_full, out_full = (
        lax.all_gather(query_weight, ("sec", "dp"), axis=0, tiled=True),
        lax.all_gather(key_weight, ("sec", "dp"), axis=0, tiled=True),
        lax.all_gather(value_weight, ("sec", "dp"), axis=0, tiled=True),
        lax.all_gather(out_weight, ("sec", "dp"), axis=0, tiled=True),
    )
    student_f = student_rows[0].astype(jnp.float32)
    inverse = lax.rsqrt(jnp.mean(student_f * student_f, axis=1, keepdims=True) + norm_eps)
    normed = (student_f * inverse * norm_gain).astype(jnp.bfloat16)
    first_pos = lax.axis_index("dp") * tok_count
    half_dim = HD // 2
    inv_freq = jnp.power(
        jnp.float32(rope_base), -2.0 * jnp.arange(half_dim, dtype=jnp.float32) / HD
    )
    positions = (first_pos + jnp.arange(tok_count, dtype=jnp.int32)).astype(jnp.float32)
    angles = positions[:, None] * inv_freq[None, :]
    cos_table = jnp.cos(angles)
    sin_table = jnp.sin(angles)
    queries = rotate(
        jnp.dot(normed, query_full, preferred_element_type=jnp.float32), cos_table, sin_table, 1.0
    ).astype(jnp.bfloat16)
    key_rows = rotate(
        jnp.dot(normed, key_full, preferred_element_type=jnp.float32), cos_table, sin_table, 1.0
    ).astype(jnp.bfloat16)
    value_rows = jnp.dot(normed, value_full, preferred_element_type=jnp.float32).astype(
        jnp.bfloat16
    )
    key_parts = [key_rows]
    value_parts = [value_rows]
    for offset in range(1, blocks_back + 1):
        earlier_keys, earlier_values = from_behind((key_rows, value_rows), "dp", offset)
        key_parts = [earlier_keys] + key_parts
        value_parts = [earlier_values] + value_parts
    key_window = jnp.concatenate(key_parts, axis=0)
    value_window = jnp.concatenate(value_parts, axis=0)
    query_pos = first_pos + jnp.arange(tok_count, dtype=jnp.int32)
    key_pos = first_pos - blocks_back * tok_count + jnp.arange(key_count, dtype=jnp.int32)
    allowed = (
        (key_pos[None, :] >= 0)
        & (key_pos[None, :] <= query_pos[:, None])
        & (key_pos[None, :] > query_pos[:, None] - W)
    )
    grouped_q = queries.reshape(tok_count, local_groups, group_size, HD)
    grouped_k = key_window.reshape(key_count, local_groups, HD)
    grouped_v = value_window.reshape(key_count, local_groups, HD)
    scores = (
        jnp.einsum("tgad,kgd->gatk", grouped_q, grouped_k, preferred_element_type=jnp.float32)
        * score_scale
    )
    scores = jnp.where(allowed, scores, masked_score)
    row_peak = jnp.max(scores, axis=3, keepdims=True)
    exp_scores = jnp.exp(scores - row_peak)
    attn_probs = exp_scores / jnp.sum(exp_scores, axis=3, keepdims=True)
    probs_b = attn_probs.astype(jnp.bfloat16)
    mixed_rows = (
        jnp.einsum("gatk,kgd->tgad", probs_b, grouped_v, preferred_element_type=jnp.float32)
        .astype(jnp.bfloat16)
        .reshape(tok_count, query_cols)
    )
    partial_value = jnp.einsum(
        "te,de->td", mixed_rows, out_full, preferred_element_type=jnp.float32
    )
    summed = lax.psum(partial_value.astype(jnp.bfloat16), "tensor").astype(jnp.float32)
    post_factor = lax.rsqrt(jnp.mean(summed * summed, axis=1, keepdims=True) + norm_eps)
    layer_full = (student_f + summed * post_factor * post_gain).astype(jnp.bfloat16)
    loss_grad = loss_scale * (layer_full.astype(jnp.float32) - target.astype(jnp.float32))
    scaled = post_gain * loss_grad
    along_sum = jnp.mean(summed * scaled, axis=1, keepdims=True)
    pre_grad = (
        post_factor * scaled - summed * post_factor * post_factor * post_factor * along_sum
    ).astype(jnp.bfloat16)
    mixed_grad = jnp.dot(pre_grad, out_full, preferred_element_type=jnp.float32).astype(
        jnp.bfloat16
    )
    grouped_g = mixed_grad.reshape(tok_count, local_groups, group_size, HD)
    prob_grad = jnp.einsum(
        "tgad,kgd->gatk", grouped_g, grouped_v, preferred_element_type=jnp.float32
    )
    score_grad = (
        attn_probs * (prob_grad - jnp.sum(attn_probs * prob_grad, axis=3, keepdims=True))
    ).astype(jnp.bfloat16)
    rotated_grad = (
        jnp.einsum(
            "gatk,kgd->tgad", score_grad, grouped_k, preferred_element_type=jnp.float32
        ).reshape(tok_count, query_cols)
        * score_scale
    )
    query_pre = rotate(rotated_grad, cos_table, sin_table, -1.0).astype(jnp.bfloat16)
    query_term = jnp.einsum("td,te->de", normed, query_pre, preferred_element_type=jnp.float32)
    out_term = jnp.einsum("td,te->de", pre_grad, mixed_rows, preferred_element_type=jnp.float32)
    grad_owned = lax.psum_scatter(
        jnp.concatenate([query_term, out_term], axis=1).astype(jnp.bfloat16),
        ("sec", "dp"),
        scatter_dimension=0,
        tiled=True,
    ).astype(jnp.float32)
    layer_share = lax.dynamic_slice_in_dim(
        layer_full, lax.axis_index("tensor") * share_cols, share_cols, 1
    )
    return (layer_share[None], grad_owned[:, :query_cols], grad_owned[:, query_cols:])


def solution(mesh):
    in_specs = (
        P("sec", "dp", None),
        P("sec", "dp", None),
        P(),
        P(),
        P(("sec", "dp"), "tensor"),
        P(("sec", "dp"), "tensor"),
        P(("sec", "dp"), "tensor"),
        P(("sec", "dp"), "tensor"),
    )
    out_specs = (P("sec", "dp", "tensor"), P(("sec", "dp"), "tensor"), P(("sec", "dp"), "tensor"))
    return jax.shard_map(shards, mesh=mesh, in_specs=in_specs, out_specs=out_specs, check_vma=False)
```

profile of v0, /device:TPU:2, one launch (start us, length us, event | category | flops | bytes accessed | tf_op | source)
XLA Modules:
  0.0 628.8 jit_solution(17924069632204809534)
XLA Ops:
  10.1 3.7 fusion.9
  16.0 53.6 %all-gather.7.cloned.1.call-done = bf16[5376,256]{1,0:T(8,128)(2,1)} async-done(((bf16[168,256]{1,0:T(8,128)(2,1)}), bf16[5376,256]{1,0:T(8,128)(2,1)}) %all-gather.7.cloned.1.call-update) | async-done | bytes 2752528 | tf_op jit(solution)/shard_map/all_gather | solution.py:72
  69.6 5.4 fusion.50
  78.4 4.0 collective-permute-start.2
  82.4 53.2 %all-gather.5.cloned.1.call-done = bf16[5376,256]{1,0:T(8,128)(2,1)} async-done(((bf16[168,256]{1,0:T(8,128)(2,1)}), bf16[5376,256]{1,0:T(8,128)(2,1)}) %all-gather.5.cloned.1.call-update) | async-done | bytes 2752528 | tf_op jit(solution)/shard_map/all_gather | solution.py:73
  135.6 5.0 fusion.53
  142.8 4.3 collective-permute-start
  147.1 57.4 %all-gather.9.cloned.1.call-done = bf16[5376,512]{1,0:T(8,128)(2,1)} async-done(((bf16[168,512]{1,0:T(8,128)(2,1)}), bf16[5376,512]{1,0:T(8,128)(2,1)}) %all-gather.9.cloned.1.call-update) | async-done | bytes 5505040 | tf_op jit(solution)/shard_map/all_gather | solution.py:71
  204.5 8.3 %copy.30 = bf16[512,5376]{1,0:T(8,128)(2,1)} copy(bf16[512,5376]{0,1:T(8,128)(2,1)} %bitcast.134) | data formatting | bytes 11010048 | tf_op jit(solution)/shard_map/dot_general | solution.py:89
  212.8 7.0 %fusion.22 = f32[512,2,256]{0,2,1:T(8,128)S(1)} fusion(bf16[2,256,5376]{2,1,0:T(8,128)(2,1)} %bitcast.135, bf16[1,512,5376]{2,1,0:T(8,128)(2,1)} %param.8, f32[5376]{0:T(1024)S(1)} %copy-done.4, f32[512]{0:T(512)S(1)} %add_rsqrt_fusion.1), kind=kOutput, calls=%fused_computation.36 | convolution fusion | flops 2829582336 | bytes 12082176 | tf_op jit(solution)/shard_map/dot_general | solution.py:89
  224.0 3.1 fusion.47
  227.1 39.8 %all-gather.11.cloned.1.call-done = bf16[5376,512]{1,0:T(8,128)(2,1)} async-done(((bf16[168,512]{1,0:T(8,128)(2,1)}), bf16[5376,512]{1,0:T(8,128)(2,1)}) %all-gather.11.cloned.1.call-update) | async-done | bytes 5505040 | tf_op jit(solution)/shard_map/all_gather | solution.py:74
  266.9 8.3 %convolution_convert_fusion.2 = bf16[512,5376]{1,0:T(8,128)(2,1)} fusion(bf16[512,512]{0,1:T(8,128)(2,1)} %bitcast.139, bf16[5376,512]{1,0:T(8,128)(2,1)} %all-gather.11.cloned.1.call-done), kind=kOutput, calls=%fused_computation.26 | convolution fusion | flops 2821324800 | bytes 11534336 | tf_op jit(solution)/shard_map/te,de->td/dot_general | solution.py:129
  276.8 110.7 %all-reduce.2.cloned.1.call-done = bf16[512,5376]{1,0:T(8,128)(2,1)} async-done(((bf16[512,5376]{1,0:T(8,128)(2,1)}), bf16[512,5376]{1,0:T(8,128)(2,1)}) %all-reduce.2.cloned.1.call-update) | async-done | bytes 5505040 | tf_op jit(solution)/shard_map/psum | solution.py:132
  387.5 3.9 fusion.15
  391.4 5.3 collective-permute-done.4
  396.7 7.1 %fusion.16 = (f32[512]{0:T(512)S(1)}, bf16[512,5376]{1,0:T(8,128)(2,1)S(1)}) fusion(bf16[512,5376]{1,0:T(8,128)(2,1)S(1)} %copy-done, bf16[512,5376]{1,0:T(8,128)(2,1)} %collective-permute-done.4, f32[5376]{0:T(1024)S(1)} %broadcast_multiply_fusion.1, f32[5376]{0:T(1024)S(1)} %copy-done.3, f32[512]{0:T(512)S(1)} %add_rsqrt_fusion, bf16[1,512,5376]{2,1,0:T(8,128)(2,1)} %param.8), kind=kLoop, calls=%fused_computation.21 | loop fusion | flops 33029632 | bytes 22067200 | tf_op jit(solution)/shard_map/reduce_sum | solution.py:137
  403.8 8.0 %fusion.8 = bf16[512,5376]{1,0:T(8,128)(2,1)S(1)} fusion(bf16[512,5376]{1,0:T(8,128)(2,1)S(1)} %copy-done, bf16[512,5376]{1,0:T(8,128)(2,1)} %collective-permute-done.4, bf16[512,5376]{1,0:T(8,128)(2,1)S(1)} %get-tuple-element.13, f32[512]{0:T(512)S(1)} %broadcast_multiply_fusion.2, f32[5376]{0:T(1024)S(1)} %broadcast_multiply_fusion.1, f32[512]{0:T(512)S(1)} %add_rsqrt_fusion), kind=kLoop, calls=%fused_computation.13 | loop fusion | flops 33030144 | bytes 22045696 | tf_op jit(solution)/shard_map/convert_element_type | solution.py:140
  411.8 3.2 convolution_convert_fusion
  415.1 5.8 convolution_convert_fusion.3
  426.2 3.6 convolution_convert_fusion.1
  429.9 5.1 pad_maximum_fusion
  435.0 14.7 %copy.48 = bf16[5376,1024]{1,0:T(8,128)(2,1)} copy(bf16[5376,1024]{0,1:T(8,128)(2,1)} %pad_maximum_fusion) | data formatting | bytes 22020096
  453.5 165.0 %reduce-scatter.4.cloned.1.call-done = bf16[168,1024]{1,0:T(8,128)(2,1)} async-done(((bf16[5376,1024]{1,0:T(8,128)(2,1)}), bf16[168,1024]{1,0:T(8,128)(2,1)}) %reduce-scatter.4.cloned.1.call-update) | async-done | bytes 344080
  (67 shorter events, 28.6 us)
Async XLA Ops:
  7.2 62.5 %copy-start.4 = (f32[5376]{0:T(1024)S(1)}, f32[5376]{0:T(1024)}, u32[]{:S(2)}) copy-start(f32[5376]{0:T(1024)} %param.10) | copy-start | bytes 64516
  7.2 62.5 %all-gather.7.cloned.1.call-start = ((), (), s32[]{:S(2)}) async-start(), calls=%async_computation.2 | async-start | bytes 2838528 | tf_op jit(solution)/shard_map/all_gather | solution.py:72
  7.9 127.7 %all-gather.5.cloned.1.call-start = ((), (), s32[]{:S(2)}) async-start(), calls=%async_computation.1 | async-start | bytes 2838528 | tf_op jit(solution)/shard_map/all_gather | solution.py:73
  8.7 195.8 %all-gather.9.cloned.1.call-start = ((), (), s32[]{:S(2)}) async-start(), calls=%async_computation.3 | async-start | bytes 5677056 | tf_op jit(solution)/shard_map/all_gather | solution.py:71
  9.4 257.5 %all-gather.11.cloned.1.call-start = ((), (), s32[]{:S(2)}) async-start(), calls=%async_computation.4 | async-start | bytes 5677056 | tf_op jit(solution)/shard_map/all_gather | solution.py:74
  10.0 377.5 %all-reduce.2.cloned.1.call-start = ((), (), s32[]{:S(2)}) async-start(), calls=%async_computation.5 | async-start | bytes 11010048 | tf_op jit(solution)/shard_map/psum | solution.py:132
  76.2 143.7 %collective-permute-start.3 = (bf16[512,256]{0,1:T(8,128)(2,1)S(1)}, bf16[512,256]{0,1:T(8,128)(2,1)S(1)}, u32[]{:S(2)}, u32[]{:S(2)}) collective-permute-start(bf16[512,256]{0,1:T(8,128)(2,1)S(1)} %maximum_bitcast_fusion.6), channel_id=1, source_target_pairs={{0,4},{4,8},{8,12},{12,16},{16,20},{20,24},{24,28},{28,32},{32,36}... | collective-permute-start | bytes 786440 | tf_op jit(solution)/shard_map/ppermute | solution.py:29
  78.4 141.6 %collective-permute-start.2 = (bf16[512,256]{0,1:T(8,128)(2,1)S(1)}, bf16[512,256]{0,1:T(8,128)(2,1)S(1)}, u32[]{:S(2)}, u32[]{:S(2)}) collective-permute-start(bf16[512,256]{0,1:T(8,128)(2,1)S(1)} %maximum_bitcast_fusion.6), channel_id=1, source_target_pairs={{0,8},{4,12},{8,16},{12,20},{16,24},{20,28},{24,32},{28,36},{32,40... | collective-permute-start | bytes 786440 | tf_op jit(solution)/shard_map/ppermute | solution.py:29
  140.7 82.2 %collective-permute-start.1 = (bf16[512,256]{1,0:T(8,128)(2,1)S(1)}, bf16[512,256]{1,0:T(8,128)(2,1)S(1)}, u32[]{:S(2)}, u32[]{:S(2)}) collective-permute-start(bf16[512,256]{1,0:T(8,128)(2,1)S(1)} %fusion.53), channel_id=1, source_target_pairs={{0,4},{4,8},{8,12},{12,16},{16,20},{20,24},{24,28},{28,32},{32,36}... | collective-permute-start | bytes 786440 | tf_op jit(solution)/shard_map/ppermute | solution.py:29
  142.8 80.1 %collective-permute-start = (bf16[512,256]{1,0:T(8,128)(2,1)S(1)}, bf16[512,256]{1,0:T(8,128)(2,1)S(1)}, u32[]{:S(2)}, u32[]{:S(2)}) collective-permute-start(bf16[512,256]{1,0:T(8,128)(2,1)S(1)} %fusion.53), channel_id=1, source_target_pairs={{0,8},{4,12},{8,16},{12,20},{16,24},{20,28},{24,32},{28,36},{32,40... | collective-permute-start | bytes 786440 | tf_op jit(solution)/shard_map/ppermute | solution.py:29
  221.4 2.7 copy-start.2
  266.9 9.9 %copy-start.3 = (f32[5376]{0:T(1024)S(1)}, f32[5376]{0:T(1024)}, u32[]{:S(2)}) copy-start(f32[5376]{0:T(1024)} %param.11) | copy-start | bytes 64516
  275.2 343.2 %reduce-scatter.4.cloned.1.call-start = ((), (), s32[]{:S(2)}) async-start(), calls=%async_computation.6 | async-start | bytes 11354112
  275.3 121.4 %collective-permute-start.4 = (bf16[512,5376]{1,0:T(8,128)(2,1)}, bf16[512,5376]{1,0:T(8,128)(2,1)}, u32[]{:S(2)}, u32[]{:S(2)}) collective-permute-start(bf16[512,5376]{1,0:T(8,128)(2,1)} %bitcast.138), channel_id=1, source_target_pairs={{0,64},{64,0},{1,65},{65,1},{2,66},{66,2},{3,67},{67,3},{4,68},{68... | collective-permute-start | bytes 16515080 | tf_op jit(solution)/shard_map/ppermute | solution.py:23
  387.5 9.2 %copy-start = (bf16[512,5376]{1,0:T(8,128)(2,1)S(1)}, bf16[512,5376]{1,0:T(8,128)(2,1)}, u32[]{:S(2)}) copy-start(bf16[512,5376]{1,0:T(8,128)(2,1)} %all-reduce.2.cloned.1.call-done) | copy-start | bytes 16515076
  403.8 8.0 %copy-start.1 = (bf16[512,5376]{1,0:T(8,128)(2,1)}, bf16[512,5376]{1,0:T(8,128)(2,1)S(1)}, u32[]{:S(2)}) copy-start(bf16[512,5376]{1,0:T(8,128)(2,1)S(1)} %get-tuple-element.13) | copy-start | bytes 16515076
  403.8 8.0 %copy-start.5 = (bf16[256,2,512]{2,0,1:T(8,128)(2,1)S(1)}, bf16[256,2,512]{2,0,1:T(8,128)(2,1)}, u32[]{:S(2)}) copy-start(bf16[256,2,512]{2,0,1:T(8,128)(2,1)} %fusion.47) | copy-start | bytes 1572868
  411.8 9.0 %slice-start.2 = ((s8[6291456]{0:T(1024)(128)(4,1)}), s8[4194304]{0:T(1024)(128)(4,1)S(1)}, s32[]{:S(2)}) async-start(s8[6291456]{0:T(1024)(128)(4,1)} %bitcast.132), calls=%async_computation.9 | async-start | bytes 8388608
  415.1 5.8 slice-start.3
  420.9 5.4 slice-start
  423.2 3.0 slice-start.1
Sparse Core Ops, SparseCore 0:
  9.7 59.8 all-gather.6
  71.3 64.2 all-gather.4
  137.3 67.1 all-gather.8
  206.1 60.8 all-gather.10
  275.3 112.1 all-reduce.1
  449.8 168.6 reduce-scatter.3
where the time goes:
time: 635 us; the launch traced here: 629 us
  waiting for transfers between devices  488 us (77%)
  matrix products  47.8 us (8%)
  other arithmetic  33.1 us (5%)
  local copies, waits for them, and re-layouts  31 us (5%)
  between operations  14.9 us (2%)
  starting transfers between devices  14.3 us (2%)
    unnamed x7, waiting for transfers between devices  168 us
    psum x1, waiting for transfers between devices, shards(): lax.psum(partial_value.astype(jnp.bfloat16), 'tensor').astype(jnp.float32)  111 us
    all_gather x1, waiting for transfers between devices, shards(): lax.all_gather(query_weight, ('sec', 'dp'), axis=0, tiled=True)  57.4 us
    all_gather x1, waiting for transfers between devices, shards(): lax.all_gather(key_weight, ('sec', 'dp'), axis=0, tiled=True)  53.6 us
    all_gather x1, waiting for transfers between devices, shards(): lax.all_gather(value_weight, ('sec', 'dp'), axis=0, tiled=True)  53.2 us
    all_gather x1, waiting for transfers between devices, shards(): lax.all_gather(out_weight, ('sec', 'dp'), axis=0, tiled=True)  39.8 us
    unnamed x24, local copies, waits for them, and re-layouts  18.9 us
  transfers between devices with their start and end apart: 11, of which 7 were waited for; matrix products, arithmetic and copies ran while one was open for 7% of the time, Pallas kernels for 0%

commit v1 on v0

--- a/solution.py
+++ b/solution.py
@@ -129,7 +129,9 @@
     partial_value = jnp.einsum(
         "te,de->td", mixed_rows, out_full, preferred_element_type=jnp.float32
     )
-    summed = lax.psum(partial_value.astype(jnp.bfloat16), "tensor").astype(jnp.float32)
+    summed = (
+        lax.all_gather(partial_value.astype(jnp.bfloat16), "tensor").sum(axis=0).astype(jnp.float32)
+    )
     post_factor = lax.rsqrt(jnp.mean(summed * summed, axis=1, keepdims=True) + norm_eps)
     layer_full = (student_f + summed * post_factor * post_gain).astype(jnp.bfloat16)
     loss_grad = loss_scale * (layer_full.astype(jnp.float32) - target.astype(jnp.float32))

time: 635 us -> 730 us (1.15)
  waiting for transfers between devices: 488 us -> 563 us
  other arithmetic: 33.1 us -> 48.7 us
    all_gather x0 -> x1, waiting for transfers between devices: none -> 195 us  [shards(): lax.all_gather(partial_value.astype(jnp.bfloat16), 'tensor').sum(axis=0)]
    psum x1 -> x0, waiting for transfers between devices: 111 us -> none  [shards(): lax.psum(partial_value.astype(jnp.bfloat16), 'tensor').astype(jnp.float32)]
    reduce_sum x0 -> x1, other arithmetic: none -> 15.6 us  [shards(): lax.all_gather(partial_value.astype(jnp.bfloat16), 'tensor').sum(axis=0)]
  transfers between devices with their start and end apart: 11 -> 11, of which waited for: 7 -> 6; matrix products, arithmetic and copies ran while one was open for 7% -> 9% of each run, Pallas kernels for 0% -> 0%
where the time goes in v1:
time: 730 us; the launch traced here: 720 us
  waiting for transfers between devices  563 us (77%)
  other arithmetic  48.7 us (7%)
  matrix products  48 us (7%)
  local copies, waits for them, and re-layouts  31.1 us (4%)
  between operations  14.7 us (2%)
  starting transfers between devices  13.9 us (2%)
    all_gather x1, waiting for transfers between devices, shards(): lax.all_gather(partial_value.astype(jnp.bfloat16), 'tensor').sum(axis=0)  195 us
    unnamed x7, waiting for transfers between devices  164 us
    all_gather x1, waiting for transfers between devices, shards(): lax.all_gather(query_weight, ('sec', 'dp'), axis=0, tiled=True)  57.4 us
    all_gather x1, waiting for transfers between devices, shards(): lax.all_gather(key_weight, ('sec', 'dp'), axis=0, tiled=True)  53.6 us
    all_gather x1, waiting for transfers between devices, shards(): lax.all_gather(value_weight, ('sec', 'dp'), axis=0, tiled=True)  53.4 us
    all_gather x1, waiting for transfers between devices, shards(): lax.all_gather(out_weight, ('sec', 'dp'), axis=0, tiled=True)  39.7 us
    unnamed x24, local copies, waits for them, and re-layouts  19.2 us
    reduce_sum x1, other arithmetic, shards(): lax.all_gather(partial_value.astype(jnp.bfloat16), 'tensor').sum(axis=0)  15.6 us
  transfers between devices with their start and end apart: 11, of which 6 were waited for; matrix products, arithmetic and copies ran while one was open for 9% of the time, Pallas kernels for 0%

profile of v1, /device:TPU:2, one launch (start us, length us, event | category | flops | bytes accessed | tf_op | source)
XLA Modules:
  0.0 719.5 jit_solution(14371583864398605268)
XLA Ops:
  10.1 3.7 fusion.9
  16.0 53.6 %all-gather.9.cloned.1.call-done = bf16[5376,256]{1,0:T(8,128)(2,1)} async-done(((bf16[168,256]{1,0:T(8,128)(2,1)}), bf16[5376,256]{1,0:T(8,128)(2,1)}) %all-gather.9.cloned.1.call-update) | async-done | bytes 2752528 | tf_op jit(solution)/shard_map/all_gather | solution.py:72
  69.6 5.4 fusion.50
  76.2 4.0 collective-permute-start.2
  82.1 53.4 %all-gather.7.cloned.1.call-done = bf16[5376,256]{1,0:T(8,128)(2,1)} async-done(((bf16[168,256]{1,0:T(8,128)(2,1)}), bf16[5376,256]{1,0:T(8,128)(2,1)}) %all-gather.7.cloned.1.call-update) | async-done | bytes 2752528 | tf_op jit(solution)/shard_map/all_gather | solution.py:73
  135.5 5.0 fusion.53
  140.6 4.0 collective-permute-start
  146.9 57.4 %all-gather.11.cloned.1.call-done = bf16[5376,512]{1,0:T(8,128)(2,1)} async-done(((bf16[168,512]{1,0:T(8,128)(2,1)}), bf16[5376,512]{1,0:T(8,128)(2,1)}) %all-gather.11.cloned.1.call-update) | async-done | bytes 5505040 | tf_op jit(solution)/shard_map/all_gather | solution.py:71
  204.3 8.0 %copy.21 = bf16[512,5376]{1,0:T(8,128)(2,1)} copy(bf16[512,5376]{0,1:T(8,128)(2,1)} %bitcast.136) | data formatting | bytes 11010048 | tf_op jit(solution)/shard_map/dot_general | solution.py:89
  212.4 7.0 fusion.22
  223.6 3.1 fusion.47
  226.7 39.7 %all-gather.13.cloned.1.call-done = bf16[5376,512]{1,0:T(8,128)(2,1)} async-done(((bf16[168,512]{1,0:T(8,128)(2,1)}), bf16[5376,512]{1,0:T(8,128)(2,1)}) %all-gather.13.cloned.1.call-update) | async-done | bytes 5505040 | tf_op jit(solution)/shard_map/all_gather | solution.py:74
  266.5 8.2 %convolution_convert_fusion.2 = bf16[512,5376]{1,0:T(8,128)(2,1)} fusion(bf16[512,512]{0,1:T(8,128)(2,1)} %bitcast.141, bf16[5376,512]{1,0:T(8,128)(2,1)} %all-gather.13.cloned.1.call-done), kind=kOutput, calls=%fused_computation.26 | convolution fusion | flops 2821324800 | bytes 11534336 | tf_op jit(solution)/shard_map/te,de->td/dot_general | solution.py:129
  276.3 195.3 %all-gather.15.cloned.1.call-done = bf16[2048,5376]{1,0:T(8,128)(2,1)} async-done(((bf16[512,5376]{1,0:T(8,128)(2,1)}), bf16[2048,5376]{1,0:T(8,128)(2,1)}) %all-gather.15.cloned.1.call-update) | async-done | bytes 22020112 | tf_op jit(solution)/shard_map/all_gather | solution.py:133
  471.5 15.6 %reduce_sum.59 = bf16[512,5376]{1,0:T(8,128)(2,1)} reduce(bf16[4,512,5376]{2,1,0:T(8,128)(2,1)} %bitcast.131, bf16[]{:T(256)} %constant.46.clone.1), dimensions={0}, to_apply=%region_3.4 | reduce | flops 8257536 | bytes 27525122 | tf_op jit(solution)/shard_map/reduce_sum | solution.py:133
  487.1 3.9 fusion.15
  491.3 7.1 fusion.16
  498.4 8.0 %fusion.8 = bf16[512,5376]{1,0:T(8,128)(2,1)S(1)} fusion(bf16[512,5376]{1,0:T(8,128)(2,1)S(1)} %copy-done, bf16[512,5376]{1,0:T(8,128)(2,1)} %collective-permute-done.4, bf16[512,5376]{1,0:T(8,128)(2,1)S(1)} %get-tuple-element.10, f32[512]{0:T(512)S(1)} %broadcast_multiply_fusion.2, f32[5376]{0:T(1024)S(1)} %broadcast_multiply_fusion.1, f32[512]{0:T(512)S(1)} %add_rsqrt_fusion), kind=kLoop, calls=%fused_computation.13 | loop fusion | flops 33030144 | bytes 22045696 | tf_op jit(solution)/shard_map/convert_element_type | solution.py:142
  506.4 3.4 convolution_convert_fusion
  509.9 5.8 convolution_convert_fusion.3
  521.1 3.6 convolution_convert_fusion.1
  524.7 5.1 pad_maximum_fusion
  529.8 14.7 %copy.39 = bf16[5376,1024]{1,0:T(8,128)(2,1)} copy(bf16[5376,1024]{0,1:T(8,128)(2,1)} %pad_maximum_fusion) | data formatting | bytes 22020096
  548.3 161.0 %reduce-scatter.4.cloned.1.call-done = bf16[168,1024]{1,0:T(8,128)(2,1)} async-done(((bf16[5376,1024]{1,0:T(8,128)(2,1)}), bf16[168,1024]{1,0:T(8,128)(2,1)}) %reduce-scatter.4.cloned.1.call-update) | async-done | bytes 344080
  (68 shorter events, 28.8 us)
Async XLA Ops:
  7.2 62.5 %copy-start.4 = (f32[5376]{0:T(1024)S(1)}, f32[5376]{0:T(1024)}, u32[]{:S(2)}) copy-start(f32[5376]{0:T(1024)} %param.10) | copy-start | bytes 64516
  7.2 62.5 %all-gather.9.cloned.1.call-start = ((), (), s32[]{:S(2)}) async-start(), calls=%async_computation.2 | async-start | bytes 2838528 | tf_op jit(solution)/shard_map/all_gather | solution.py:72
  7.9 127.6 %all-gather.7.cloned.1.call-start = ((), (), s32[]{:S(2)}) async-start(), calls=%async_computation.1 | async-start | bytes 2838528 | tf_op jit(solution)/shard_map/all_gather | solution.py:73
  8.7 195.7 %all-gather.11.cloned.1.call-start = ((), (), s32[]{:S(2)}) async-start(), calls=%async_computation.3 | async-start | bytes 5677056 | tf_op jit(solution)/shard_map/all_gather | solution.py:71
  9.4 257.1 %all-gather.13.cloned.1.call-start = ((), (), s32[]{:S(2)}) async-start(), calls=%async_computation.4 | async-start | bytes 5677056 | tf_op jit(solution)/shard_map/all_gather | solution.py:74
  10.0 461.6 %all-gather.15.cloned.1.call-start = ((), (), s32[]{:S(2)}) async-start(), calls=%async_computation.5 | async-start | bytes 27525120 | tf_op jit(solution)/shard_map/all_gather | solution.py:133
  76.2 143.3 %collective-permute-start.2 = (bf16[512,256]{0,1:T(8,128)(2,1)S(1)}, bf16[512,256]{0,1:T(8,128)(2,1)S(1)}, u32[]{:S(2)}, u32[]{:S(2)}) collective-permute-start(bf16[512,256]{0,1:T(8,128)(2,1)S(1)} %maximum_bitcast_fusion.6), channel_id=1, source_target_pairs={{0,8},{4,12},{8,16},{12,20},{16,24},{20,28},{24,32},{28,36},{32,40... | collective-permute-start | bytes 786440 | tf_op jit(solution)/shard_map/ppermute | solution.py:29
  80.2 139.3 %collective-permute-start.3 = (bf16[512,256]{0,1:T(8,128)(2,1)S(1)}, bf16[512,256]{0,1:T(8,128)(2,1)S(1)}, u32[]{:S(2)}, u32[]{:S(2)}) collective-permute-start(bf16[512,256]{0,1:T(8,128)(2,1)S(1)} %maximum_bitcast_fusion.6), channel_id=1, source_target_pairs={{0,4},{4,8},{8,12},{12,16},{16,20},{20,24},{24,28},{28,32},{32,36}... | collective-permute-start | bytes 786440 | tf_op jit(solution)/shard_map/ppermute | solution.py:29
  140.6 81.9 %collective-permute-start = (bf16[512,256]{1,0:T(8,128)(2,1)S(1)}, bf16[512,256]{1,0:T(8,128)(2,1)S(1)}, u32[]{:S(2)}, u32[]{:S(2)}) collective-permute-start(bf16[512,256]{1,0:T(8,128)(2,1)S(1)} %fusion.53), channel_id=1, source_target_pairs={{0,8},{4,12},{8,16},{12,20},{16,24},{20,28},{24,32},{28,36},{32,40... | collective-permute-start | bytes 786440 | tf_op jit(solution)/shard_map/ppermute | solution.py:29
  144.6 77.9 %collective-permute-start.1 = (bf16[512,256]{1,0:T(8,128)(2,1)S(1)}, bf16[512,256]{1,0:T(8,128)(2,1)S(1)}, u32[]{:S(2)}, u32[]{:S(2)}) collective-permute-start(bf16[512,256]{1,0:T(8,128)(2,1)S(1)} %fusion.53), channel_id=1, source_target_pairs={{0,4},{4,8},{8,12},{12,16},{16,20},{20,24},{24,28},{28,32},{32,36}... | collective-permute-start | bytes 786440 | tf_op jit(solution)/shard_map/ppermute | solution.py:29
  221.0 2.7 copy-start.2
  266.5 9.8 %copy-start.3 = (f32[5376]{0:T(1024)S(1)}, f32[5376]{0:T(1024)}, u32[]{:S(2)}) copy-start(f32[5376]{0:T(1024)} %param.11) | copy-start | bytes 64516
  274.7 434.6 %reduce-scatter.4.cloned.1.call-start = ((), (), s32[]{:S(2)}) async-start(), calls=%async_computation.6 | async-start | bytes 11354112
  274.8 216.2 %collective-permute-start.4 = (bf16[512,5376]{1,0:T(8,128)(2,1)}, bf16[512,5376]{1,0:T(8,128)(2,1)}, u32[]{:S(2)}, u32[]{:S(2)}) collective-permute-start(bf16[512,5376]{1,0:T(8,128)(2,1)} %bitcast.140), channel_id=1, source_target_pairs={{0,64},{64,0},{1,65},{65,1},{2,66},{66,2},{3,67},{67,3},{4,68},{68... | collective-permute-start | bytes 16515080 | tf_op jit(solution)/shard_map/ppermute | solution.py:23
  487.1 4.2 copy-start
  498.4 8.0 %copy-start.1 = (bf16[512,5376]{1,0:T(8,128)(2,1)}, bf16[512,5376]{1,0:T(8,128)(2,1)S(1)}, u32[]{:S(2)}) copy-start(bf16[512,5376]{1,0:T(8,128)(2,1)S(1)} %get-tuple-element.10) | copy-start | bytes 16515076
  498.4 8.0 %copy-start.5 = (bf16[256,2,512]{2,0,1:T(8,128)(2,1)S(1)}, bf16[256,2,512]{2,0,1:T(8,128)(2,1)}, u32[]{:S(2)}) copy-start(bf16[256,2,512]{2,0,1:T(8,128)(2,1)} %fusion.47) | copy-start | bytes 1572868
  506.4 9.2 %slice-start.2 = ((s8[6291456]{0:T(1024)(128)(4,1)}), s8[4194304]{0:T(1024)(128)(4,1)S(1)}, s32[]{:S(2)}) async-start(s8[6291456]{0:T(1024)(128)(4,1)} %bitcast.134), calls=%async_computation.9 | async-start | bytes 8388608
  509.9 5.8 slice-start.3
  515.7 5.4 slice-start
  518.0 3.0 slice-start.1
Sparse Core Ops, SparseCore 0:
  9.7 59.8 all-gather.8
  71.3 64.1 all-gather.6
  137.2 67.0 all-gather.10
  205.9 60.5 all-gather.12
  274.8 196.6 all-gather.14
  544.6 164.6 reduce-scatter.3
